TPU v7x, 32 devices: a whole 2x2x4 slice. The times are simulated.
32 devices in a mesh: depth: 8 (over y, x, core), row: 4 (over z).
Axes of the slice: x: 2, y: 2, z: 4, core: 2. Of those that a mesh axis runs over, the one named last changes fastest.
Arguments:
- input_cells: bfloat16 [32, 64, 128, 128], P('depth', 'row'), may hold values from -6 to 6
- first_weight: bfloat16 [3, 3, 3, 64, 128], P(None, None, None, None, 'depth'), may hold values from -0.15625 to 0.15625
- second_weight: bfloat16 [3, 3, 3, 128, 256], P(None, None, None, None, 'depth'), may hold values from -0.109375 to 0.109375
Outputs:
- encoded: bfloat16 [8, 16, 32, 512], P('depth', 'row')
All inputs are finite; a program needn't handle non-finite values.
Results may differ from a plain program's by a relative error of at most 0.0049.
Values may be sent and summed in bfloat16 or wider, within the bound.
A program may use at most 64 MiB of HBM per device.

v0:
```python
import jax
import jax.numpy as jnp
from jax import lax
from jax.sharding import PartitionSpec as P


def from_behind(x, axis, by):
    count = lax.axis_size(axis)
    pairs = [(i, i + by) for i in range(count) if 0 <= i + by < count]
    return lax.ppermute(x, axis, pairs)


def stacked(weight, depth_tap, row_tap):
    kernel_taps = weight[depth_tap, row_tap]
    zeros_block = jnp.zeros_like(kernel_taps[0])
    upper_part = jnp.concatenate([kernel_taps[1], kernel_taps[2]], 0)
    lower_part = jnp.concatenate([zeros_block, kernel_taps[0]], 0)
    return jnp.concatenate([upper_part, lower_part], 1)


def convolve(extended, weight):
    planes = extended.shape[0] - 1
    row_count = extended.shape[1] - 1
    pair_count = extended.shape[2]
    features = extended.shape[3]
    out_width = weight.shape[4]
    running = jnp.zeros((planes // 2 * (row_count // 2) * pair_count, 2 * out_width), jnp.float32)
    for depth_tap in range(3):
        for row_tap in range(3):
            window = extended[depth_tap : depth_tap + planes : 2, row_tap : row_tap + row_count : 2]
            running = running + jnp.dot(
                window.reshape(-1, features),
                stacked(weight, depth_tap, row_tap),
                preferred_element_type=jnp.float32,
            )
    running = running.reshape(planes // 2, row_count // 2, pair_count, 2 * out_width)
    carried = jnp.pad(running[:, :, :-1, out_width:], ((0, 0), (0, 0), (1, 0), (0, 0)))
    return running[..., :out_width] + carried


def finish(field):
    activated = jnp.maximum(field, 0.0).astype(jnp.bfloat16)
    shape_now = activated.shape
    return activated.reshape(shape_now[0], shape_now[1], shape_now[2] // 2, 2 * shape_now[3])


def per_device(input_cells, first_weight, second_weight):
    first_full, second_full = (
        lax.all_gather(first_weight, "depth", axis=4, tiled=True),
        lax.all_gather(second_weight, "depth", axis=4, tiled=True),
    )
    below_plane = from_behind(input_cells[-1:], "depth", 1)
    with_plane = jnp.concatenate([below_plane, input_cells], 0)
    below_row = from_behind(with_plane[:, -1:], "row", 1)
    extended = jnp.concatenate([below_row, with_plane], 1)
    hidden = finish(convolve(extended, first_full))
    hidden_below = from_behind(hidden[-1:], "depth", 1)
    hidden_plus = jnp.concatenate([hidden_below, hidden], 0)
    hidden_rowrim = from_behind(hidden_plus[:, -1:], "row", 1)
    hidden_ext = jnp.concatenate([hidden_rowrim, hidden_plus], 1)
    summed = convolve(hidden_ext, second_full)
    return finish(summed)


def solution(mesh):
    return jax.shard_map(
        per_device,
        mesh=mesh,
        in_specs=(
            P("depth", "row", None, None),
            P(None, None, None, None, "depth"),
            P(None, None, None, None, "depth"),
        ),
        out_specs=P("depth", "row", None, None),
        check_vma=False,
    )
```

profile of v0, /device:TPU:22, one launch (start us, length us, event | category | flops | bytes accessed | tf_op | source)
XLA Modules:
  0.0 72.2 jit_solution(71455804238040424)
XLA Ops:
  6.5 0.7 all-gather.2.cloned.1.call-update
  7.3 1.1 %slice.378 = bf16[1,16,128,128]{3,2,1,0:T(8,128)(2,1)S(1)} slice(bf16[4,16,128,128]{3,2,1,0:T(8,128)(2,1)} %param.3), slice={[3:4], [0:16], [0:128], [0:128]} | slice | bytes 1048576 | tf_op jit(solution)/shard_map/slice | solution.py:52
  8.4 2.1 %collective-permute-start = (bf16[1,16,128,128]{3,2,1,0:T(8,128)(2,1)S(1)}, bf16[1,16,128,128]{3,2,1,0:T(8,128)(2,1)S(1)}, u32[]{:S(2)}, u32[]{:S(2)}) collective-permute-start(bf16[1,16,128,128]{3,2,1,0:T(8,128)(2,1)S(1)} %slice.378), channel_id=1, source_target_pairs={{0,4},{4,8},{8,12},{12,16},{16,20},{20,24},{24,28},{1,5},{5,9},{9,... | collective-permute-start | bytes 1572872 | tf_op jit(solution)/shard_map/ppermute | solution.py:10
  10.4 1.7 %fusion.230 = (bf16[2,8,128,128]{3,2,1,0:T(8,128)(2,1)S(1)}, bf16[2,8,128,128]{3,2,1,0:T(8,128)(2,1)S(1)}, bf16[2,8,128,128]{3,2,1,0:T(8,128)(2,1)S(1)}, bf16[2,8,128,128]{3,2,1,0:T(8,128)(2,1)S(1)}) fusion(bf16[4,16,128,128]{3,2,1,0:T(8,128)(2,1)} %param.3), kind=kLoop, calls=%fused_computation.291 | loop fusion | bytes 4194304 | tf_op jit(solution)/shard_map/slice | solution.py:30
  12.1 19.7 %all_gather.6 = bf16[3,3,3,64,128]{3,4,2,1,0:T(8,128)(2,1)S(1)} all-gather(bf16[3,3,3,64,16]{3,4,2,1,0:T(8,128)(2,1)S(1)} %copy-done.2), channel_id=1, replica_groups=mesh['depth'=8,'row'=4] {'depth'}, dimensions={4}, use_global_device_ids=true | all-gather | bytes 497664 | tf_op jit(solution)/shard_map/all_gather | solution.py:49
  31.9 0.5 convolution_bitcast_fusion.3
  32.4 0.5 convolution_bitcast_fusion.1
  33.0 1.0 %copy-done = bf16[4,16,128,128]{3,2,1,0:T(8,128)(2,1)S(1)} copy-done((bf16[4,16,128,128]{3,2,1,0:T(8,128)(2,1)S(1)}, bf16[4,16,128,128]{3,2,1,0:T(8,128)(2,1)}, u32[]{:S(2)}) %copy-start) | copy-done | bytes 2097176
  34.0 0.3 constant_dynamic-update-slice_fusion
  34.4 3.5 %collective-permute-start.1 = (bf16[5,1,128,128]{3,2,1,0:T(8,128)(2,1)S(1)}, bf16[5,1,128,128]{3,2,1,0:T(8,128)(2,1)S(1)}, u32[]{:S(2)}, u32[]{:S(2)}) collective-permute-start(bf16[5,1,128,128]{3,2,1,0:T(8,128)(2,1)S(1)} %slice.459), channel_id=1, source_target_pairs={{0,1},{1,2},{2,3},{4,5},{5,6},{6,7},{8,9},{9,10},{10,11},{12,13},{... | collective-permute-start | bytes 491528 | tf_op jit(solution)/shard_map/ppermute | solution.py:10
  37.9 0.5 fusion.106
  38.4 0.5 fusion.103
  38.9 3.8 %collective-permute-done.1 = bf16[5,1,128,128]{3,2,1,0:T(8,128)(2,1)S(1)} collective-permute-done((bf16[5,1,128,128]{3,2,1,0:T(8,128)(2,1)S(1)}, bf16[5,1,128,128]{3,2,1,0:T(8,128)(2,1)S(1)}, u32[]{:S(2)}, u32[]{:S(2)}) %collective-permute-start.1) | collective-permute-done | bytes 163872 | tf_op jit(solution)/shard_map/ppermute | solution.py:10
  43.2 0.5 fusion.4
  43.7 0.5 fusion.3
  44.2 0.5 fusion
  44.8 0.6 fusion.2
  45.4 0.5 fusion.1
  46.3 1.9 %collective-permute-start.2 = (bf16[1,8,64,256]{3,2,1,0:T(8,128)(2,1)S(1)}, bf16[1,8,64,256]{3,2,1,0:T(8,128)(2,1)S(1)}, u32[]{:S(2)}, u32[]{:S(2)}) collective-permute-start(bf16[1,8,64,256]{3,2,1,0:T(8,128)(2,1)S(1)} %slice.419), channel_id=1, source_target_pairs={{0,4},{4,8},{8,12},{12,16},{16,20},{20,24},{24,28},{1,5},{5,9},{9,... | collective-permute-start | bytes 786440 | tf_op jit(solution)/shard_map/ppermute | solution.py:10
  48.5 5.5 %collective-permute-done.2 = bf16[1,8,64,256]{3,2,1,0:T(8,128)(2,1)S(1)} collective-permute-done((bf16[1,8,64,256]{3,2,1,0:T(8,128)(2,1)S(1)}, bf16[1,8,64,256]{3,2,1,0:T(8,128)(2,1)S(1)}, u32[]{:S(2)}, u32[]{:S(2)}) %collective-permute-start.2) | collective-permute-done | bytes 262176 | tf_op jit(solution)/shard_map/ppermute | solution.py:10
  54.1 3.5 %collective-permute-start.3 = (bf16[3,1,64,256]{3,2,1,0:T(8,128)(2,1)S(1)}, bf16[3,1,64,256]{3,2,1,0:T(8,128)(2,1)S(1)}, u32[]{:S(2)}, u32[]{:S(2)}) collective-permute-start(bf16[3,1,64,256]{3,2,1,0:T(8,128)(2,1)S(1)} %slice.490), channel_id=1, source_target_pairs={{0,1},{1,2},{2,3},{4,5},{5,6},{6,7},{8,9},{9,10},{10,11},{12,13},{... | collective-permute-start | bytes 294920 | tf_op jit(solution)/shard_map/ppermute | solution.py:10
  57.6 3.0 %collective-permute-done.3 = bf16[3,1,64,256]{3,2,1,0:T(8,128)(2,1)S(1)} collective-permute-done((bf16[3,1,64,256]{3,2,1,0:T(8,128)(2,1)S(1)}, bf16[3,1,64,256]{3,2,1,0:T(8,128)(2,1)S(1)}, u32[]{:S(2)}, u32[]{:S(2)}) %collective-permute-start.3) | collective-permute-done | bytes 98336 | tf_op jit(solution)/shard_map/ppermute | solution.py:10
  60.8 1.2 %slice_bitcast_fusion.20 = (bf16[128,256]{0,1:T(8,128)(2,1)S(1)}, bf16[128,256]{0,1:T(8,128)(2,1)S(1)}, bf16[128,256]{0,1:T(8,128)(2,1)S(1)}, bf16[128,256]{0,1:...) fusion(bf16[3,3,3,128,256]{3,4,2,1,0:T(8,128)(2,1)} %all-gather, ...), kind=kLoop, calls=%fused_computation.143 | loop fusion | bytes 1048576 | tf_op jit(solution)/shard_map/squeeze | solution.py:16
  62.3 0.3 convolution_add_fusion.10
  62.7 0.3 convolution_add_fusion.9
  62.9 0.3 convolution_add_fusion.8
  63.2 0.3 convolution_add_fusion.7
  63.5 0.3 convolution_add_fusion.6
  63.8 0.3 convolution_add_fusion.5
  64.0 0.3 convolution_add_fusion.4
  64.3 0.3 convolution_add_fusion.3
  64.6 0.7 reshape.196
  (31 shorter events, 1.9 us)
Async XLA Ops:
  6.5 54.2 %all-gather.2.cloned.1.call-start = ((), (), s32[]{:S(2)}) async-start(), calls=%async_computation | async-start | bytes 1990656 | tf_op jit(solution)/shard_map/all_gather | solution.py:50
  8.3 3.8 %copy-start.2 = (bf16[3,3,3,64,16]{3,4,2,1,0:T(8,128)(2,1)S(1)}, bf16[3,3,3,64,16]{3,4,2,1,0:T(8,128)(2,1)}, u32[]{:S(2)}) copy-start(bf16[3,3,3,64,16]{3,4,2,1,0:T(8,128)(2,1)} %param.4) | copy-start | bytes 165892
  8.4 24.6 %collective-permute-start = (bf16[1,16,128,128]{3,2,1,0:T(8,128)(2,1)S(1)}, bf16[1,16,128,128]{3,2,1,0:T(8,128)(2,1)S(1)}, u32[]{:S(2)}, u32[]{:S(2)}) collective-permute-start(bf16[1,16,128,128]{3,2,1,0:T(8,128)(2,1)S(1)} %slice.378), channel_id=1, source_target_pairs={{0,4},{4,8},{8,12},{12,16},{16,20},{20,24},{24,28},{1,5},{5,9},{9,... | collective-permute-start | bytes 1572872 | tf_op jit(solution)/shard_map/ppermute | solution.py:10
  32.4 1.6 %copy-start = (bf16[4,16,128,128]{3,2,1,0:T(8,128)(2,1)S(1)}, bf16[4,16,128,128]{3,2,1,0:T(8,128)(2,1)}, u32[]{:S(2)}) copy-start(bf16[4,16,128,128]{3,2,1,0:T(8,128)(2,1)} %param.3) | copy-start | bytes 6291460
  34.4 8.3 %collective-permute-start.1 = (bf16[5,1,128,128]{3,2,1,0:T(8,128)(2,1)S(1)}, bf16[5,1,128,128]{3,2,1,0:T(8,128)(2,1)S(1)}, u32[]{:S(2)}, u32[]{:S(2)}) collective-permute-start(bf16[5,1,128,128]{3,2,1,0:T(8,128)(2,1)S(1)} %slice.459), channel_id=1, source_target_pairs={{0,1},{1,2},{2,3},{4,5},{5,6},{6,7},{8,9},{9,10},{10,11},{12,13},{... | collective-permute-start | bytes 491528 | tf_op jit(solution)/shard_map/ppermute | solution.py:10
  46.3 7.7 %collective-permute-start.2 = (bf16[1,8,64,256]{3,2,1,0:T(8,128)(2,1)S(1)}, bf16[1,8,64,256]{3,2,1,0:T(8,128)(2,1)S(1)}, u32[]{:S(2)}, u32[]{:S(2)}) collective-permute-start(bf16[1,8,64,256]{3,2,1,0:T(8,128)(2,1)S(1)} %slice.419), channel_id=1, source_target_pairs={{0,4},{4,8},{8,12},{12,16},{16,20},{20,24},{24,28},{1,5},{5,9},{9,... | collective-permute-start | bytes 786440 | tf_op jit(solution)/shard_map/ppermute | solution.py:10
  54.1 6.5 %collective-permute-start.3 = (bf16[3,1,64,256]{3,2,1,0:T(8,128)(2,1)S(1)}, bf16[3,1,64,256]{3,2,1,0:T(8,128)(2,1)S(1)}, u32[]{:S(2)}, u32[]{:S(2)}) collective-permute-start(bf16[3,1,64,256]{3,2,1,0:T(8,128)(2,1)S(1)} %slice.490), channel_id=1, source_target_pairs={{0,1},{1,2},{2,3},{4,5},{5,6},{6,7},{8,9},{9,10},{10,11},{12,13},{... | collective-permute-start | bytes 294920 | tf_op jit(solution)/shard_map/ppermute | solution.py:10
  60.8 1.8 %copy-start.1 = (bf16[3,3,3,128,256]{3,4,2,1,0:T(8,128)(2,1)S(1)}, bf16[3,3,3,128,256]{3,4,2,1,0:T(8,128)(2,1)}, u32[]{:S(2)}) copy-start(bf16[3,3,3,128,256]{3,4,2,1,0:T(8,128)(2,1)} %all-gather.2.cloned.1.call-done) | copy-start | bytes 5308420
Sparse Core Ops, SparseCore 0:
  9.2 28.6 all-gather.1
where the time goes:
time: 72.5 us; the launch traced here: 72.2 us
  blocking collectives  19.7 us (27%)
  between operations  13.8 us (19%)
  waiting for transfers between devices  13.1 us (18%)
  starting transfers between devices  10.9 us (15%)
  matrix products  7.11 us (10%)
  local copies, waits for them, and re-layouts  7.02 us (10%)
    all_gather x1, blocking collectives, per_device(): lax.all_gather(first_weight, 'depth', axis=4, tiled=True)  19.7 us
    ppermute x4, waiting for transfers between devices, from_behind(): return lax.ppermute(x, axis, pairs)  12.4 us
    ppermute x4, starting transfers between devices, from_behind(): return lax.ppermute(x, axis, pairs)  10.9 us
    dot_general x18, matrix products, convolve(): jnp.dot(window.reshape(-1, features), stacked(weight, depth_tap, row_tap)...  7.11 us
    slice x6, local copies, waits for them, and re-layouts, convolve(): extended[depth_tap:depth_tap + planes:2, row_tap:row_tap + row_count:2]  2.07 us
  transfers between devices with their start and end apart: 5, of which 3 were waited for; matrix products, arithmetic and copies ran while one was open for 13% of the time, Pallas kernels for 0%

commit v1 on v0

--- a/solution.py
+++ b/solution.py
@@ -2,6 +2,12 @@
 import jax.numpy as jnp
 from jax import lax
 from jax.sharding import PartitionSpec as P
+
+
+def stack_and_merge(x, axis, dim):
+    terms = lax.all_gather(x, axis, axis=0, tiled=False)
+    whole = jnp.concatenate(terms, axis=dim)
+    return whole
 
 
 def from_behind(x, axis, by):
@@ -46,7 +52,7 @@
 
 def per_device(input_cells, first_weight, second_weight):
     first_full, second_full = (
-        lax.all_gather(first_weight, "depth", axis=4, tiled=True),
+        stack_and_merge(first_weight, "depth", 4),
         lax.all_gather(second_weight, "depth", axis=4, tiled=True),
     )
     below_plane = from_behind(input_cells[-1:], "depth", 1)

time: 72.5 us -> 68.3 us (0.942)
  blocking collectives: 19.7 us -> 14.7 us
  local copies, waits for them, and re-layouts: 7.02 us -> 8.21 us
    all_gather x1, blocking collectives: 19.7 us -> 14.7 us  [stack_and_merge(): terms = lax.all_gather(x, axis, axis=0, tiled=False)]
  transfers between devices with their start and end apart: 5 -> 5, of which waited for: 3 -> 3; matrix products, arithmetic and copies ran while one was open for 13% -> 15% of each run, Pallas kernels for 0% -> 0%
where the time goes in v1:
time: 68.3 us; the launch traced here: 67.7 us
  blocking collectives  14.7 us (22%)
  between operations  13.8 us (20%)
  waiting for transfers between devices  12.4 us (18%)
  starting transfers between devices  10.9 us (16%)
  local copies, waits for them, and re-layouts  8.21 us (12%)
  matrix products  7.07 us (10%)
    all_gather x1, blocking collectives, stack_and_merge(): terms = lax.all_gather(x, axis, axis=0, tiled=False)  14.7 us
    ppermute x4, waiting for transfers between devices, from_behind(): return lax.ppermute(x, axis, pairs)  11.7 us
    ppermute x4, starting transfers between devices, from_behind(): return lax.ppermute(x, axis, pairs)  10.9 us
    dot_general x18, matrix products, convolve(): jnp.dot(window.reshape(-1, features), stacked(weight, depth_tap, row_tap)...  7.07 us
    slice x6, local copies, waits for them, and re-layouts, convolve(): extended[depth_tap:depth_tap + planes:2, row_tap:row_tap + row_count:2]  2.78 us
    squeeze x4, local copies, waits for them, and re-layouts, stacked(): upper_part = jnp.concatenate([kernel_taps[1], kernel_taps[2]], 0)  1.38 us
  transfers between devices with their start and end apart: 5, of which 3 were waited for; matrix products, arithmetic and copies ran while one was open for 15% of the time, Pallas kernels for 0%

profile of v1, /device:TPU:22, one launch (start us, length us, event | category | flops | bytes accessed | tf_op | source)
XLA Modules:
  0.0 67.7 jit_solution(13232055000347203651)
XLA Ops:
  6.5 0.7 %all-gather.3.cloned.1.call-update = ((bf16[3,3,3,128,32]{3,4,2,1,0:T(8,128)(2,1)}), bf16[3,3,3,128,256]{3,4,2,1,0:T(8,128)(2,1)}) async-update(((), (), s32[]{:S(2)}) %all-gather.3.cloned.1.call-start, bf16[3,3,3,128,32]{3,4,2,1,0:T(8,128)(2,1)} %param.5) | async-update | bytes 2211864
  7.3 1.1 %slice.378 = bf16[1,16,128,128]{3,2,1,0:T(8,128)(2,1)S(1)} slice(bf16[4,16,128,128]{3,2,1,0:T(8,128)(2,1)} %param.3), slice={[3:4], [0:16], [0:128], [0:128]} | slice | bytes 1048576 | tf_op jit(solution)/shard_map/slice | solution.py:58
  8.4 2.1 %collective-permute-start = (bf16[1,16,128,128]{3,2,1,0:T(8,128)(2,1)S(1)}, bf16[1,16,128,128]{3,2,1,0:T(8,128)(2,1)S(1)}, u32[]{:S(2)}, u32[]{:S(2)}) collective-permute-start(bf16[1,16,128,128]{3,2,1,0:T(8,128)(2,1)S(1)} %slice.378), channel_id=1, source_target_pairs={{0,4},{4,8},{8,12},{12,16},{16,20},{20,24},{24,28},{1,5},{5,9},{9,... | collective-permute-start | bytes 1572872 | tf_op jit(solution)/shard_map/ppermute | solution.py:16
  10.4 1.7 %fusion.230 = (bf16[2,8,128,128]{3,2,1,0:T(8,128)(2,1)S(1)}, bf16[2,8,128,128]{3,2,1,0:T(8,128)(2,1)S(1)}, bf16[2,8,128,128]{3,2,1,0:T(8,128)(2,1)S(1)}, bf16[2,8,128,128]{3,2,1,0:T(8,128)(2,1)S(1)}) fusion(bf16[4,16,128,128]{3,2,1,0:T(8,128)(2,1)} %param.3), kind=kLoop, calls=%fused_computation.291 | loop fusion | bytes 4194304 | tf_op jit(solution)/shard_map/slice | solution.py:36
  12.2 14.7 %all-gather = bf16[24,3,3,64,16]{3,4,2,1,0:T(8,128)(2,1)S(1)} all-gather(bf16[3,3,3,64,16]{3,4,2,1,0:T(8,128)(2,1)S(1)} %copy-done.5), channel_id=2, replica_groups=mesh['depth'=8,'row'=4] {'depth'}, dimensions={0}, use_global_device_ids=true | all-gather | bytes 497664 | tf_op jit(solution)/shard_map/all_gather | solution.py:8
  27.1 0.5 convolution_bitcast_fusion.3
  27.7 0.5 convolution_bitcast_fusion.1
  28.3 1.0 %copy-done = bf16[4,16,128,128]{3,2,1,0:T(8,128)(2,1)S(1)} copy-done((bf16[4,16,128,128]{3,2,1,0:T(8,128)(2,1)S(1)}, bf16[4,16,128,128]{3,2,1,0:T(8,128)(2,1)}, u32[]{:S(2)}) %copy-start) | copy-done | bytes 2097176
  29.2 0.3 constant_dynamic-update-slice_fusion
  29.6 3.5 %collective-permute-start.1 = (bf16[5,1,128,128]{3,2,1,0:T(8,128)(2,1)S(1)}, bf16[5,1,128,128]{3,2,1,0:T(8,128)(2,1)S(1)}, u32[]{:S(2)}, u32[]{:S(2)}) collective-permute-start(bf16[5,1,128,128]{3,2,1,0:T(8,128)(2,1)S(1)} %slice.459), channel_id=1, source_target_pairs={{0,1},{1,2},{2,3},{4,5},{5,6},{6,7},{8,9},{9,10},{10,11},{12,13},{... | collective-permute-start | bytes 491528 | tf_op jit(solution)/shard_map/ppermute | solution.py:16
  33.1 0.5 fusion.106
  33.6 0.5 fusion.103
  34.1 3.8 %collective-permute-done.1 = bf16[5,1,128,128]{3,2,1,0:T(8,128)(2,1)S(1)} collective-permute-done((bf16[5,1,128,128]{3,2,1,0:T(8,128)(2,1)S(1)}, bf16[5,1,128,128]{3,2,1,0:T(8,128)(2,1)S(1)}, u32[]{:S(2)}, u32[]{:S(2)}) %collective-permute-start.1) | collective-permute-done | bytes 163872 | tf_op jit(solution)/shard_map/ppermute | solution.py:16
  38.4 0.5 fusion.4
  38.9 0.5 fusion.3
  39.5 0.5 fusion
  40.0 0.6 fusion.2
  40.6 0.5 fusion.1
  41.6 1.9 %collective-permute-start.2 = (bf16[1,8,64,256]{3,2,1,0:T(8,128)(2,1)S(1)}, bf16[1,8,64,256]{3,2,1,0:T(8,128)(2,1)S(1)}, u32[]{:S(2)}, u32[]{:S(2)}) collective-permute-start(bf16[1,8,64,256]{3,2,1,0:T(8,128)(2,1)S(1)} %slice.419), channel_id=1, source_target_pairs={{0,4},{4,8},{8,12},{12,16},{16,20},{20,24},{24,28},{1,5},{5,9},{9,... | collective-permute-start | bytes 786440 | tf_op jit(solution)/shard_map/ppermute | solution.py:16
  43.7 0.7 %fusion.233 = (bf16[1,4,64,256]{3,2,1,0:T(8,128)(2,1)S(1)}, bf16[1,4,64,256]{3,2,1,0:T(8,128)(2,1)}, bf16[1,4,64,256]{3,2,1,0:T(8,128)(2,1)}, bf16[1,4,64,256]{3,2,1,0:T(8,128)(2,1)}) fusion(bf16[2,8,64,256]{3,2,1,0:T(8,128)(2,1)S(1)} %reshape.193), kind=kLoop, calls=%fused_computation.294 | loop fusion | bytes 1048576 | tf_op jit(solution)/shard_map/slice | solution.py:36
  44.5 4.8 %collective-permute-done.2 = bf16[1,8,64,256]{3,2,1,0:T(8,128)(2,1)S(1)} collective-permute-done((bf16[1,8,64,256]{3,2,1,0:T(8,128)(2,1)S(1)}, bf16[1,8,64,256]{3,2,1,0:T(8,128)(2,1)S(1)}, u32[]{:S(2)}, u32[]{:S(2)}) %collective-permute-start.2) | collective-permute-done | bytes 262176 | tf_op jit(solution)/shard_map/ppermute | solution.py:16
  49.4 3.5 %collective-permute-start.3 = (bf16[3,1,64,256]{3,2,1,0:T(8,128)(2,1)S(1)}, bf16[3,1,64,256]{3,2,1,0:T(8,128)(2,1)S(1)}, u32[]{:S(2)}, u32[]{:S(2)}) collective-permute-start(bf16[3,1,64,256]{3,2,1,0:T(8,128)(2,1)S(1)} %slice.490), channel_id=1, source_target_pairs={{0,1},{1,2},{2,3},{4,5},{5,6},{6,7},{8,9},{9,10},{10,11},{12,13},{... | collective-permute-start | bytes 294920 | tf_op jit(solution)/shard_map/ppermute | solution.py:16
  52.9 3.0 %collective-permute-done.3 = bf16[3,1,64,256]{3,2,1,0:T(8,128)(2,1)S(1)} collective-permute-done((bf16[3,1,64,256]{3,2,1,0:T(8,128)(2,1)S(1)}, bf16[3,1,64,256]{3,2,1,0:T(8,128)(2,1)S(1)}, u32[]{:S(2)}, u32[]{:S(2)}) %collective-permute-start.3) | collective-permute-done | bytes 98336 | tf_op jit(solution)/shard_map/ppermute | solution.py:16
  56.0 1.2 %slice_bitcast_fusion.20 = (bf16[128,256]{0,1:T(8,128)(2,1)S(1)}, bf16[128,256]{0,1:T(8,128)(2,1)S(1)}, bf16[128,256]{0,1:T(8,128)(2,1)S(1)}, bf16[128,256]{0,1:...) fusion(bf16[3,3,3,128,256]{3,4,2,1,0:T(8,128)(2,1)} %all-gather, ...), kind=kLoop, calls=%fused_computation.143 | loop fusion | bytes 1048576 | tf_op jit(solution)/shard_map/squeeze | solution.py:22
  57.5 0.3 convolution_add_fusion.10
  57.9 0.3 convolution_add_fusion.9
  58.2 0.3 convolution_add_fusion.8
  58.7 0.3 convolution_add_fusion.7
  59.0 0.3 convolution_add_fusion.6
  59.3 0.3 convolution_add_fusion.5
  59.8 0.3 convolution_add_fusion.3
  60.2 0.7 %reshape.204 = bf16[1,4,32,512]{3,2,1,0:T(8,128)(2,1)} reshape(bf16[1,4,64,256]{3,2,1,0:T(8,128)(2,1)S(1)} %fusion.36) | data formatting | bytes 262144 | tf_op jit(solution)/shard_map/reshape | solution.py:50
  (38 shorter events, 2.6 us)
Async XLA Ops:
  6.5 49.5 %all-gather.3.cloned.1.call-start = ((), (), s32[]{:S(2)}) async-start(), calls=%async_computation | async-start | bytes 1990656 | tf_op jit(solution)/shard_map/all_gather | solution.py:56
  8.3 3.8 %copy-start.5 = (bf16[3,3,3,64,16]{3,4,2,1,0:T(8,128)(2,1)S(1)}, bf16[3,3,3,64,16]{3,4,2,1,0:T(8,128)(2,1)}, u32[]{:S(2)}) copy-start(bf16[3,3,3,64,16]{3,4,2,1,0:T(8,128)(2,1)} %param.4) | copy-start | bytes 165892
  8.4 19.8 %collective-permute-start = (bf16[1,16,128,128]{3,2,1,0:T(8,128)(2,1)S(1)}, bf16[1,16,128,128]{3,2,1,0:T(8,128)(2,1)S(1)}, u32[]{:S(2)}, u32[]{:S(2)}) collective-permute-start(bf16[1,16,128,128]{3,2,1,0:T(8,128)(2,1)S(1)} %slice.378), channel_id=1, source_target_pairs={{0,4},{4,8},{8,12},{12,16},{16,20},{20,24},{24,28},{1,5},{5,9},{9,... | collective-permute-start | bytes 1572872 | tf_op jit(solution)/shard_map/ppermute | solution.py:16
  27.6 1.6 %copy-start = (bf16[4,16,128,128]{3,2,1,0:T(8,128)(2,1)S(1)}, bf16[4,16,128,128]{3,2,1,0:T(8,128)(2,1)}, u32[]{:S(2)}) copy-start(bf16[4,16,128,128]{3,2,1,0:T(8,128)(2,1)} %param.3) | copy-start | bytes 6291460
  29.6 8.4 %collective-permute-start.1 = (bf16[5,1,128,128]{3,2,1,0:T(8,128)(2,1)S(1)}, bf16[5,1,128,128]{3,2,1,0:T(8,128)(2,1)S(1)}, u32[]{:S(2)}, u32[]{:S(2)}) collective-permute-start(bf16[5,1,128,128]{3,2,1,0:T(8,128)(2,1)S(1)} %slice.459), channel_id=1, source_target_pairs={{0,1},{1,2},{2,3},{4,5},{5,6},{6,7},{8,9},{9,10},{10,11},{12,13},{... | collective-permute-start | bytes 491528 | tf_op jit(solution)/shard_map/ppermute | solution.py:16
  41.6 7.7 %collective-permute-start.2 = (bf16[1,8,64,256]{3,2,1,0:T(8,128)(2,1)S(1)}, bf16[1,8,64,256]{3,2,1,0:T(8,128)(2,1)S(1)}, u32[]{:S(2)}, u32[]{:S(2)}) collective-permute-start(bf16[1,8,64,256]{3,2,1,0:T(8,128)(2,1)S(1)} %slice.419), channel_id=1, source_target_pairs={{0,4},{4,8},{8,12},{12,16},{16,20},{20,24},{24,28},{1,5},{5,9},{9,... | collective-permute-start | bytes 786440 | tf_op jit(solution)/shard_map/ppermute | solution.py:16
  49.4 6.5 %collective-permute-start.3 = (bf16[3,1,64,256]{3,2,1,0:T(8,128)(2,1)S(1)}, bf16[3,1,64,256]{3,2,1,0:T(8,128)(2,1)S(1)}, u32[]{:S(2)}, u32[]{:S(2)}) collective-permute-start(bf16[3,1,64,256]{3,2,1,0:T(8,128)(2,1)S(1)} %slice.490), channel_id=1, source_target_pairs={{0,1},{1,2},{2,3},{4,5},{5,6},{6,7},{8,9},{9,10},{10,11},{12,13},{... | collective-permute-start | bytes 294920 | tf_op jit(solution)/shard_map/ppermute | solution.py:16
  56.0 1.8 %copy-start.1 = (bf16[3,3,3,128,256]{3,4,2,1,0:T(8,128)(2,1)S(1)}, bf16[3,3,3,128,256]{3,4,2,1,0:T(8,128)(2,1)}, u32[]{:S(2)}) copy-start(bf16[3,3,3,128,256]{3,4,2,1,0:T(8,128)(2,1)} %all-gather.3.cloned.1.call-done) | copy-start | bytes 5308420
  57.8 0.9 %copy-start.4 = (bf16[1,4,64,256]{3,2,1,0:T(8,128)(2,1)S(1)}, bf16[1,4,64,256]{3,2,1,0:T(8,128)(2,1)}, u32[]{:S(2)}) copy-start(bf16[1,4,64,256]{3,2,1,0:T(8,128)(2,1)} %get-tuple-element.76) | copy-start | bytes 393220
  57.9 1.1 %copy-start.3 = (bf16[1,4,64,256]{3,2,1,0:T(8,128)(2,1)S(1)}, bf16[1,4,64,256]{3,2,1,0:T(8,128)(2,1)}, u32[]{:S(2)}) copy-start(bf16[1,4,64,256]{3,2,1,0:T(8,128)(2,1)} %get-tuple-element.75) | copy-start | bytes 393220
  58.5 1.1 %copy-start.2 = (bf16[1,4,64,256]{3,2,1,0:T(8,128)(2,1)S(1)}, bf16[1,4,64,256]{3,2,1,0:T(8,128)(2,1)}, u32[]{:S(2)}) copy-start(bf16[1,4,64,256]{3,2,1,0:T(8,128)(2,1)} %get-tuple-element.74) | copy-start | bytes 393220
Sparse Core Ops, SparseCore 0:
  9.2 28.3 all-gather.2
